TPU v7x, 32 devices: a whole 2x2x4 slice. The times are simulated.
32 devices in a mesh: seq: 4 (over x, core), fsdp: 8 (over z, y).
Axes of the slice: x: 2, y: 2, z: 4, core: 2. Of those that a mesh axis runs over, the one named last changes fastest.
Arguments:
- tokens: bfloat16 [8, 1024, 1536], P('fsdp', 'seq'), may hold values from -6 to 6
- cotangent: bfloat16 [8, 1024, 1536], P('fsdp', 'seq'), may hold values from -6 to 6
- doc_lengths: int32 [8, 8], P('fsdp'), may hold values from 1 to 512, 1024 in all within a row
- w_qkv: float32 [1536, 2048], P(('seq', 'fsdp')), may hold values from -0.15625 to 0.15625
- w_out: float32 [1536, 1536], P(('seq', 'fsdp')), may hold values from -1.5 to 1.5
- w_gate_up: float32 [1536, 17920], P(('seq', 'fsdp')), may hold values from -0.15625 to 0.15625
- w_down: float32 [8960, 1536], P(('seq', 'fsdp')), may hold values from -0.0625 to 0.0625
- small_params: float32 [5120], P(('seq', 'fsdp')), may hold values from -2 to 4.5
- first_qkv: float32 [1536, 2048], P(('seq', 'fsdp')), may hold values from -0.66 to 0.66
- first_out: float32 [1536, 1536], P(('seq', 'fsdp')), may hold values from -0.66 to 0.66
- first_gate_up: float32 [1536, 17920], P(('seq', 'fsdp')), may hold values from -0.66 to 0.66
- first_down: float32 [8960, 1536], P(('seq', 'fsdp')), may hold values from -0.66 to 0.66
- first_small: float32 [5120], P(('seq', 'fsdp')), may hold values from -0.66 to 0.66
- second_qkv: float32 [1536, 2048], P(('seq', 'fsdp')), may hold values from 0.001 to 0.004
- second_out: float32 [1536, 1536], P(('seq', 'fsdp')), may hold values from 0.001 to 0.004
- second_gate_up: float32 [1536, 17920], P(('seq', 'fsdp')), may hold values from 0.001 to 0.004
- second_down: float32 [8960, 1536], P(('seq', 'fsdp')), may hold values from 0.001 to 0.004
- second_small: float32 [5120], P(('seq', 'fsdp')), may hold values from 0.001 to 0.004
Outputs:
- block_out: bfloat16 [8, 1024, 1536], P('fsdp', 'seq')
- tokens_grad: bfloat16 [8, 1024, 1536], P('fsdp', 'seq')
- grad_norm: float32 [], replicated
- matrix_norms: float32 [2, 12], replicated
- updated_qkv: float32 [1536, 2048], P(('seq', 'fsdp'))
- updated_out: float32 [1536, 1536], P(('seq', 'fsdp'))
- updated_gate_up: float32 [1536, 17920], P(('seq', 'fsdp'))
- updated_down: float32 [8960, 1536], P(('seq', 'fsdp'))
- updated_small: float32 [5120], P(('seq', 'fsdp'))
- mean_qkv: float32 [1536, 2048], P(('seq', 'fsdp'))
- mean_out: float32 [1536, 1536], P(('seq', 'fsdp'))
- mean_gate_up: float32 [1536, 17920], P(('seq', 'fsdp'))
- mean_down: float32 [8960, 1536], P(('seq', 'fsdp'))
- mean_small: float32 [5120], P(('seq', 'fsdp'))
- square_qkv: float32 [1536, 2048], P(('seq', 'fsdp'))
- square_out: float32 [1536, 1536], P(('seq', 'fsdp'))
- square_gate_up: float32 [1536, 17920], P(('seq', 'fsdp'))
- square_down: float32 [8960, 1536], P(('seq', 'fsdp'))
- square_small: float32 [5120], P(('seq', 'fsdp'))
Inputs may be any that keep to these rules, and one draw needn't show every extreme that they name: `doc_lengths`: the lengths of a row sum to 1024.
All inputs are finite; a program needn't handle non-finite values.
Results may differ from a plain program's by a relative error of at most 0.015.
The roundings to bfloat16 on the way count: a program that leaves them out, or rounds other values in their place, can miss the bound.
Values may be sent and summed in bfloat16 or wider, within the bound.
A program may use at most 512 MiB of HBM per device.

v0:
```python
from functools import partial
import math

import jax
import jax.numpy as jnp
from jax import lax
from jax.sharding import PartitionSpec as P

D = 1536
HEADS = 12
KV_HEADS = 2
HEAD_DIM = 128
FF = 8960
QKV = 2048
NPARAMS = 46797824


eps_norm = 1e-06
rope_base = 10000.0
beta_one = 0.9
beta_two = 0.999
lamb_eps = 1e-06
decay_rate = 0.01
learn_rate = 1.0
step_count = 10
trust_eps = 1e-06
masked_score = -1e30
piece_count = 12


def normed(values, gain):
    factor = lax.rsqrt(jnp.mean(values * values, axis=-1, keepdims=True) + eps_norm)
    return values * factor * gain


def rope_tables(positions, width):
    half = width // 2
    freq = jnp.exp(jnp.arange(half).astype(jnp.float32) * (-2.0 * math.log(rope_base) / width))
    angle = positions.astype(jnp.float32)[:, None] * freq[None, :]
    angle = jnp.concatenate([angle, angle], axis=-1)
    return (jnp.cos(angle)[:, None, :], jnp.sin(angle)[:, None, :])


def rope_turn(values, cosine, sine):
    half = values.shape[-1] // 2
    turned = jnp.concatenate([-values[..., half:], values[..., :half]], axis=-1)
    return values * cosine + turned * sine


def swish_product(gate, upper):
    return jax.nn.silu(gate) * upper


def doc_starts(lengths, places):
    ends = jnp.cumsum(lengths)
    return jnp.sum(jnp.where(ends[None, :] <= places[:, None], lengths[None, :], 0), axis=1)


def contract_rows(left, right):
    return lax.dot_general(
        left, right, (((0,), (0,)), ((), ())), preferred_element_type=jnp.float32
    )


def contract_cols(left, right):
    return lax.dot_general(
        left, right, (((1,), (1,)), ((), ())), preferred_element_type=jnp.float32
    )


def part_labels(count, bounds, first, offset):
    index = offset + jnp.arange(count)
    label = jnp.full((count,), first, jnp.int32)
    for bound in bounds:
        label = label + (index >= bound).astype(jnp.int32)
    return label


def piece_sums(values, labels):
    onehot = labels[:, None] == jnp.arange(piece_count)[None, :]
    return jnp.sum(jnp.where(onehot, values[:, None], 0.0), axis=0)


def column_squares(values):
    if values.ndim == 1:
        return values * values
    return jnp.sum(values * values, axis=0)


def spread_trust(trust, labels):
    onehot = labels[:, None] == jnp.arange(piece_count)[None, :]
    return jnp.sum(jnp.where(onehot, trust[None, :], 0.0), axis=1)


def shards(
    tokens,
    cotangent,
    doc_lengths,
    w_qkv,
    w_out,
    w_gate_up,
    w_down,
    small_params,
    first_qkv,
    first_out,
    first_gate_up,
    first_down,
    first_small,
    second_qkv,
    second_out,
    second_gate_up,
    second_down,
    second_small,
):
    heads_width = HEADS * HEAD_DIM
    kv_width = KV_HEADS * HEAD_DIM
    group = HEADS // KV_HEADS
    score_scale = 1.0 / math.sqrt(HEAD_DIM)
    qkv_full, out_full, small_full = (
        lax.all_gather(w_qkv.astype(jnp.bfloat16), ("seq", "fsdp"), axis=0, tiled=True),
        lax.all_gather(w_out.astype(jnp.bfloat16), ("seq", "fsdp"), axis=0, tiled=True),
        lax.all_gather(small_params.astype(jnp.bfloat16), ("seq", "fsdp"), axis=0, tiled=True),
    )
    small_wide = small_full.astype(jnp.float32)
    bias = small_wide[:QKV]
    gain_one = small_wide[QKV : QKV + D]
    gain_two = small_wide[QKV + D :]
    inputs = tokens[0].astype(jnp.float32)
    rows = inputs.shape[0]
    length = rows * lax.axis_size("seq")
    places = lax.axis_index("seq") * rows + jnp.arange(rows)
    key_places = jnp.arange(length)
    starts = doc_starts(doc_lengths[0], places)
    allowed = (key_places[None, :] <= places[:, None]) & (key_places[None, :] >= starts[:, None])
    cosine, sine = rope_tables(places - starts, HEAD_DIM)
    normed_one = normed(inputs, gain_one).astype(jnp.bfloat16)
    projected = jnp.dot(normed_one, qkv_full, preferred_element_type=jnp.float32) + bias
    query_raw = projected[:, :heads_width].reshape(rows, HEADS, HEAD_DIM)
    key_raw = projected[:, heads_width : heads_width + kv_width].reshape(rows, KV_HEADS, HEAD_DIM)
    value_low = projected[:, heads_width + kv_width :].astype(jnp.bfloat16)
    query_low = rope_turn(query_raw, cosine, sine).astype(jnp.bfloat16)
    key_low = rope_turn(key_raw, cosine, sine).astype(jnp.bfloat16).reshape(rows, kv_width)
    kv_rows = lax.all_gather(
        jnp.concatenate([key_low, value_low], axis=1), "seq", axis=0, tiled=True
    )
    keys_grouped = kv_rows[:, :kv_width].reshape(length, KV_HEADS, HEAD_DIM).transpose(1, 0, 2)
    values_grouped = kv_rows[:, kv_width:].reshape(length, KV_HEADS, HEAD_DIM).transpose(1, 0, 2)
    query_grouped = query_low.reshape(rows, KV_HEADS, group, HEAD_DIM).transpose(1, 0, 2, 3)

    def attend_forward(parts):
        block_query, block_keys, block_values = parts
        scores = (
            jnp.einsum("tgd,kd->tgk", block_query, block_keys, preferred_element_type=jnp.float32)
            * score_scale
        )
        scores = jnp.where(allowed[:, None, :], scores, masked_score)
        highest = jnp.max(scores, axis=-1, keepdims=True)
        weights = jnp.exp(scores - highest)
        totals = jnp.sum(weights, axis=-1, keepdims=True)
        probs_low = (weights / totals).astype(jnp.bfloat16)
        mixed = jnp.einsum(
            "tgk,kd->tgd", probs_low, block_values, preferred_element_type=jnp.float32
        )
        return (mixed, (highest + jnp.log(totals))[..., 0])

    mixed, log_totals = lax.map(attend_forward, (query_grouped, keys_grouped, values_grouped))
    mixed_low = mixed.transpose(1, 0, 2, 3).reshape(rows, heads_width).astype(jnp.bfloat16)
    middle = inputs + jnp.dot(mixed_low, out_full, preferred_element_type=jnp.float32)
    normed_two = normed(middle, gain_two).astype(jnp.bfloat16)
    cot_low = cotangent[0]
    gate_up_full, down_full = (
        lax.all_gather(w_gate_up.astype(jnp.bfloat16), ("seq", "fsdp"), axis=0, tiled=True),
        lax.all_gather(w_down.astype(jnp.bfloat16), ("seq", "fsdp"), axis=0, tiled=True),
    )
    gate_up = jnp.dot(normed_two, gate_up_full, preferred_element_type=jnp.float32)
    hidden, swish_back = jax.vjp(swish_product, gate_up[:, :FF], gate_up[:, FF:])
    hidden_low = hidden.astype(jnp.bfloat16)
    mlp_term = jnp.dot(hidden_low, down_full, preferred_element_type=jnp.float32)
    d_hidden = contract_cols(cot_low, down_full)
    d_gate, d_upper = swish_back(d_hidden)
    d_gate_up = jnp.concatenate([d_gate, d_upper], axis=1).astype(jnp.bfloat16)
    d_normed_two = contract_cols(d_gate_up, gate_up_full)
    grad_down = lax.psum_scatter(
        contract_rows(hidden_low, cot_low), ("seq", "fsdp"), scatter_dimension=0, tiled=True
    )
    grad_gate_up = lax.psum_scatter(
        contract_rows(normed_two, d_gate_up), ("seq", "fsdp"), scatter_dimension=0, tiled=True
    )
    block_out = (middle + mlp_term).astype(jnp.bfloat16)[None]
    unused_two, norm_two_back = jax.vjp(normed, middle, gain_two)
    d_middle_norm, d_gain_two = norm_two_back(d_normed_two)
    d_middle = cot_low.astype(jnp.float32) + d_middle_norm
    d_branch_low = d_middle.astype(jnp.bfloat16)
    grad_out_term = contract_rows(mixed_low, d_branch_low)
    d_mixed_low = contract_cols(d_branch_low, out_full).astype(jnp.bfloat16)
    d_mixed_grouped = d_mixed_low.reshape(rows, KV_HEADS, group, HEAD_DIM).transpose(1, 0, 2, 3)

    def attend_back(parts):
        block_query, block_keys, block_values, block_grad, block_log = parts
        scores = (
            jnp.einsum("tgd,kd->tgk", block_query, block_keys, preferred_element_type=jnp.float32)
            * score_scale
        )
        scores = jnp.where(allowed[:, None, :], scores, masked_score)
        probs = jnp.exp(scores - block_log[..., None])
        probs_low = probs.astype(jnp.bfloat16)
        d_probs = jnp.einsum(
            "tgd,kd->tgk", block_grad, block_values, preferred_element_type=jnp.float32
        )
        d_values = jnp.einsum(
            "tgk,tgd->kd", probs_low, block_grad, preferred_element_type=jnp.float32
        )
        centre = jnp.sum(probs * d_probs, axis=-1, keepdims=True)
        d_scores = (probs * (d_probs - centre)).astype(jnp.bfloat16)
        d_query = (
            jnp.einsum("tgk,kd->tgd", d_scores, block_keys, preferred_element_type=jnp.float32)
            * score_scale
        )
        d_keys = (
            jnp.einsum("tgk,tgd->kd", d_scores, block_query, preferred_element_type=jnp.float32)
            * score_scale
        )
        return (d_query, d_keys, d_values)

    d_query, d_keys, d_values = lax.map(
        attend_back, (query_grouped, keys_grouped, values_grouped, d_mixed_grouped, log_totals)
    )
    d_kv_rows = jnp.concatenate(
        [
            d_keys.transpose(1, 0, 2).reshape(length, kv_width),
            d_values.transpose(1, 0, 2).reshape(length, kv_width),
        ],
        axis=1,
    )
    d_kv_local = lax.psum_scatter(
        d_kv_rows.astype(jnp.bfloat16), "seq", scatter_dimension=0, tiled=True
    ).astype(jnp.float32)
    unused_query, rope_query_back = jax.vjp(partial(rope_turn, cosine=cosine, sine=sine), query_raw)
    unused_key, rope_key_back = jax.vjp(partial(rope_turn, cosine=cosine, sine=sine), key_raw)
    (d_query_raw,) = rope_query_back(d_query.transpose(1, 0, 2, 3).reshape(rows, HEADS, HEAD_DIM))
    (d_key_raw,) = rope_key_back(d_kv_local[:, :kv_width].reshape(rows, KV_HEADS, HEAD_DIM))
    d_projected = jnp.concatenate(
        [
            d_query_raw.reshape(rows, heads_width),
            d_key_raw.reshape(rows, kv_width),
            d_kv_local[:, kv_width:],
        ],
        axis=1,
    ).astype(jnp.bfloat16)
    d_bias = jnp.sum(d_projected.astype(jnp.float32), axis=0)
    grad_qkv_term = contract_rows(normed_one, d_projected)
    d_normed_one = contract_cols(d_projected, qkv_full)
    unused_one, norm_one_back = jax.vjp(normed, inputs, gain_one)
    d_inputs, d_gain_one = norm_one_back(d_normed_one)
    tokens_grad = (d_middle + d_inputs).astype(jnp.bfloat16)[None]
    grad_qkv, grad_out, grad_small = (
        lax.psum_scatter(grad_qkv_term, ("seq", "fsdp"), scatter_dimension=0, tiled=True),
        lax.psum_scatter(grad_out_term, ("seq", "fsdp"), scatter_dimension=0, tiled=True),
        lax.psum_scatter(
            jnp.concatenate([d_bias, d_gain_one, d_gain_two]),
            ("seq", "fsdp"),
            scatter_dimension=0,
            tiled=True,
        ),
    )
    masters = (w_qkv, w_out, w_gate_up, w_down, small_params)
    grads = (grad_qkv, grad_out, grad_gate_up, grad_down, grad_small)
    firsts = (first_qkv, first_out, first_gate_up, first_down, first_small)
    seconds = (second_qkv, second_out, second_gate_up, second_down, second_small)
    small_offset = lax.axis_index(("seq", "fsdp")) * small_params.shape[0]
    labels = (
        part_labels(QKV, [heads_width, heads_width + kv_width], 0, 0),
        part_labels(D, [], 3, 0),
        part_labels(2 * FF, [FF], 4, 0),
        part_labels(D, [], 6, 0),
        part_labels(
            small_params.shape[0],
            [heads_width, heads_width + kv_width, QKV, QKV + D],
            7,
            small_offset,
        ),
    )
    grad_local = jnp.sum(jnp.stack([jnp.sum(grad * grad) for grad in grads]))
    weight_local = jnp.sum(
        jnp.stack(
            [piece_sums(column_squares(master), label) for master, label in zip(masters, labels)]
        ),
        axis=0,
    )
    grad_total, weight_total = lax.psum((grad_local, weight_local), ("seq", "fsdp"))
    grad_norm = jnp.sqrt(grad_total)
    factor = jnp.minimum(1.0, math.sqrt(NPARAMS) / grad_norm)
    results = []
    for master, grad, first, second in zip(masters, grads, firsts, seconds):
        clipped = grad * factor
        first_new = beta_one * first + (1.0 - beta_one) * clipped
        second_new = beta_two * second + (1.0 - beta_two) * clipped * clipped
        update = (
            first_new
            / (1.0 - beta_one**step_count)
            / (jnp.sqrt(second_new / (1.0 - beta_two**step_count)) + lamb_eps)
            + decay_rate * master
        )
        results.append((first_new, second_new, update))
    update_local = jnp.sum(
        jnp.stack(
            [piece_sums(column_squares(item[2]), label) for item, label in zip(results, labels)]
        ),
        axis=0,
    )
    update_total = lax.psum(update_local, ("seq", "fsdp"))
    weight_norm = jnp.sqrt(weight_total)
    update_norm = jnp.sqrt(update_total)
    trust = weight_norm / (update_norm + trust_eps)
    updated = [
        master - learn_rate * spread_trust(trust, label) * item[2]
        for master, item, label in zip(masters, results, labels)
    ]
    matrix_norms = jnp.stack([weight_norm, update_norm])
    return (
        block_out,
        tokens_grad,
        grad_norm,
        matrix_norms,
        updated[0],
        updated[1],
        updated[2],
        updated[3],
        updated[4],
        results[0][0],
        results[1][0],
        results[2][0],
        results[3][0],
        results[4][0],
        results[0][1],
        results[1][1],
        results[2][1],
        results[3][1],
        results[4][1],
    )


def solution(mesh):
    return jax.shard_map(
        shards,
        mesh=mesh,
        in_specs=(
            P("fsdp", "seq", None),
            P("fsdp", "seq", None),
            P("fsdp", None),
            P(("seq", "fsdp"), None),
            P(("seq", "fsdp"), None),
            P(("seq", "fsdp"), None),
            P(("seq", "fsdp"), None),
            P(("seq", "fsdp")),
            P(("seq", "fsdp"), None),
            P(("seq", "fsdp"), None),
            P(("seq", "fsdp"), None),
            P(("seq", "fsdp"), None),
            P(("seq", "fsdp")),
            P(("seq", "fsdp"), None),
            P(("seq", "fsdp"), None),
            P(("seq", "fsdp"), None),
            P(("seq", "fsdp"), None),
            P(("seq", "fsdp")),
        ),
        out_specs=(
            P("fsdp", "seq", None),
            P("fsdp", "seq", None),
            P(),
            P(),
            P(("seq", "fsdp"), None),
            P(("seq", "fsdp"), None),
            P(("seq", "fsdp"), None),
            P(("seq", "fsdp"), None),
            P(("seq", "fsdp")),
            P(("seq", "fsdp"), None),
            P(("seq", "fsdp"), None),
            P(("seq", "fsdp"), None),
            P(("seq", "fsdp"), None),
            P(("seq", "fsdp")),
            P(("seq", "fsdp"), None),
            P(("seq", "fsdp"), None),
            P(("seq", "fsdp"), None),
            P(("seq", "fsdp"), None),
            P(("seq", "fsdp")),
        ),
        check_vma=False,
    )
```

profile of v0, /device:TPU:0, one launch (start us, length us, event | category | flops | bytes accessed | tf_op | source)
XLA Modules:
  0.0 2568.6 jit_solution(3238549616355298390)
XLA Ops:
  10.0 42.4 %all-reduce.4 = bf16[5120]{0:T(1024)(128)(2,1)S(1)} all-reduce(bf16[5120]{0:T(1024)(128)(2,1)S(1)} %dynamic-update-slice), channel_id=1, replica_groups=mesh['seq'=4,'fsdp'=8] {'seq','fsdp'}, use_global_device_ids=true, to_apply=%add.4 | all-reduce | flops 5120 | bytes 20480
  58.2 25.9 %all-gather.6.cloned.1.call-done = bf16[1536,2048]{1,0:T(8,128)(2,1)} async-done(((bf16[48,2048]{1,0:T(8,128)(2,1)}), bf16[1536,2048]{1,0:T(8,128)(2,1)}) %all-gather.6.cloned.1.call-update) | async-done | bytes 6291472 | tf_op jit(solution)/shard_map/all_gather | solution.py:120
  113.2 7.6 all-gather.8.cloned.1.call-done
  122.5 11.8 while.28
  134.3 53.8 %all-gather.10.cloned.1.call-done = bf16[1536,1536]{1,0:T(8,128)(2,1)} async-done(((bf16[48,1536]{1,0:T(8,128)(2,1)}), bf16[1536,1536]{1,0:T(8,128)(2,1)}) %all-gather.10.cloned.1.call-update) | async-done | bytes 4718608 | tf_op jit(solution)/shard_map/all_gather | solution.py:121
  192.4 296.4 %all-gather.12.cloned.1.call-done = bf16[1536,17920]{1,0:T(8,128)(2,1)} async-done(((bf16[48,17920]{1,0:T(8,128)(2,1)}), bf16[1536,17920]{1,0:T(8,128)(2,1)}) %all-gather.12.cloned.1.call-update) | async-done | bytes 55050256 | tf_op jit(solution)/shard_map/all_gather | solution.py:172
  488.8 30.0 %fusion.108 = f32[256,17920]{1,0:T(8,128)} fusion(bf16[1536,17920]{1,0:T(8,128)(2,1)} %all-gather.12.cloned.1.call-done, f32[256,1536]{1,0:T(8,128)S(1)} %get-tuple-element.361, f32[1536]{0:T(1024)S(1)} %get-tuple-element.354, f32[256]{0:T(256)S(1)} %fusion.105), kind=kOutput, calls=%fused_computation.231 | convolution fusion | flops 14094041088 | bytes 74980352 | tf_op jit(solution)/shard_map/dot_general | solution.py:175
  518.7 137.5 %all-gather.14.cloned.1.call-done = bf16[8960,1536]{1,0:T(8,128)(2,1)} async-done(((bf16[280,1536]{1,0:T(8,128)(2,1)}), bf16[8960,1536]{1,0:T(8,128)(2,1)}) %all-gather.14.cloned.1.call-update) | async-done | bytes 27525136 | tf_op jit(solution)/shard_map/all_gather | solution.py:173
  656.3 21.8 fusion.61
  678.1 25.8 %multiply_reduce_fusion.7 = (f32[1536]{0:T(1024)}, f32[256]{0:T(256)S(1)}, f32[256,1536]{1,0:T(8,128)}) fusion(f32[256,1536]{1,0:T(8,128)S(1)} %get-tuple-element.361, f32[256]{0:T(256)S(1)} %fusion.105, f32[1536]{0:T(1024)S(1)} %get-tuple-element.354, bf16[1536,17920]{1,0:T(8,128)(2,1)} %all-gather.12.cloned.1.call-done, ...), kind=kOutput, calls=%fused_computation.124 | convolution fusion | flops 14113568768 | bytes 67385344 | tf_op jit(solution)/shard_map/dot_general | solution.py:66
  713.9 34.1 %while.29 = (s32[]{:T(128)}, f32[2,256,6,128]{3,1,2,0:T(8,128)}, bf16[2,1024,128]{1,2,0:T(8,128)(2,1)}, bf16[2,1024,128]{1,2,0:T(8,128)(2,1)}, bf16[2,256,6,128]...) while((s32[]{:T(128)}, f32[2,256,6,128]{3,1,2,0:T(8,128)}, ...), condition=%wide.region_11.12_spmd.clone, body=%wide.region_9.11_spmd.clone.sunk | while | flops 2038102528 | bytes 96258320 | solution.py:225
  761.2 12.4 reduce-scatter.8.cloned.1.call-done
  777.7 7.4 fusion.94
  785.1 25.0 fusion.85
  810.4 42.5 %fusion.63 = f32[1536,17920]{1,0:T(8,128)} fusion(bf16[256,8960]{1,0:T(8,128)(2,1)} %get-tuple-element.338, bf16[256,8960]{1,0:T(8,128)(2,1)} %get-tuple-element.337, f32[256,1536]{1,0:T(8,128)S(1)} %get-tuple-element.361, f32[1536]{0:T(1024)S(1)} %get-tuple-element.354, f32[256]{0:T(256)S(1)} %fusion.105), kind=kOutput, calls=%fused_computation.76 | convolution fusion | flops 14112391168 | bytes 120855552 | tf_op jit(solution)/shard_map/dot_general | solution.py:60
  854.0 15.4 fusion.67
  875.7 41.4 %all-reduce.6 = f32[5120]{0:T(1024)S(1)} all-reduce(f32[5120]{0:T(1024)S(1)} %pad_maximum_fusion.7), channel_id=7, replica_groups=mesh['seq'=4,'fsdp'=8] {'seq','fsdp'}, use_global_device_ids=true, to_apply=%region_25.26.clone | all-reduce | flops 5120 | bytes 40960
  919.4 158.2 %reduce-scatter.10.cloned.1.call-done = f32[48,2048]{1,0:T(8,128)} async-done(((f32[1536,2048]{1,0:T(8,128)}), f32[48,2048]{1,0:T(8,128)}) %reduce-scatter.10.cloned.1.call-update) | async-done | bytes 393232 | tf_op jit(solution)/shard_map/reduce_scatter | solution.py:257
  1080.5 466.0 %reduce-scatter.16.cloned.1.call-done = f32[280,1536]{1,0:T(8,128)} async-done(((f32[8960,1536]{1,0:T(8,128)}), f32[280,1536]{1,0:T(8,128)}) %reduce-scatter.16.cloned.1.call-update) | async-done | bytes 1720336
  1549.0 889.1 %reduce-scatter.14.cloned.1.call-done = f32[48,17920]{1,0:T(8,128)} async-done(((f32[1536,17920]{1,0:T(8,128)}), f32[48,17920]{1,0:T(8,128)}) %reduce-scatter.14.cloned.1.call-update) | async-done | bytes 3440656 | tf_op jit(solution)/shard_map/reduce_scatter | solution.py:186
  2443.5 39.6 %psum.21 = f32[]{:T(128)} all-reduce(f32[]{:T(128)S(6)} %reduce_sum.430), channel_id=1, replica_groups=mesh['seq'=4,'fsdp'=8] {'seq','fsdp'}, use_global_device_ids=true, to_apply=%region_27.28 | all-reduce | flops 1 | bytes 8 | tf_op jit(solution)/shard_map/psum | solution.py:290
  2491.8 7.1 multiply_reduce_fusion.2
  2504.7 40.2 %all-reduce.7 = (f32[12]{0:T(128)S(1)}, f32[12]{0:T(128)S(1)}) all-reduce(f32[12]{0:T(128)S(1)} %copy-done.56, f32[12]{0:T(128)} %add_add_fusion.3), channel_id=1, replica_groups=mesh['seq'=4,'fsdp'=8] {'seq','fsdp'}, use_global_device_ids=true, to_apply=%region_47.48 | all-reduce | flops 24 | bytes 192 | tf_op jit(solution)/shard_map/psum | solution.py:311
  2551.6 6.7 multiply_subtract_fusion
  (277 shorter events, 155.8 us)
Async XLA Ops:
  7.2 76.9 %copy-start.8 = (bf16[1,256,1536]{2,1,0:T(8,128)(2,1)S(1)}, bf16[1,256,1536]{2,1,0:T(8,128)(2,1)}, u32[]{:S(2)}) copy-start(bf16[1,256,1536]{2,1,0:T(8,128)(2,1)} %param.22) | copy-start | bytes 2359300
  7.2 76.9 %all-gather.6.cloned.1.call-start = ((), (), s32[]{:S(2)}) async-start(), calls=%async_computation.5 | async-start | bytes 6488064 | tf_op jit(solution)/shard_map/all_gather | solution.py:120
  9.0 111.8 %all-gather.8.cloned.1.call-start = ((), (), s32[]{:S(2)}) async-start(), calls=%async_computation.6 | async-start | bytes 1310720 | tf_op jit(solution)/shard_map/all_gather | solution.py:143
  55.2 33.5 %copy-start.36 = (f32[256,128]{1,0:T(8,128)}, f32[256,128]{1,0:T(8,128)S(1)}, u32[]{:S(2)}) copy-start(f32[256,128]{1,0:T(8,128)S(1)} %get-tuple-element.352) | copy-start | bytes 393220
  55.3 33.4 %copy-start.25 = (f32[256,128]{0,1:T(8,128)}, f32[256,128]{0,1:T(8,128)S(1)}, u32[]{:S(2)}) copy-start(f32[256,128]{0,1:T(8,128)S(1)} %copy.123) | copy-start | bytes 393220
  58.2 30.6 %copy-start.43 = (f32[256]{0:T(256)}, f32[256]{0:T(256)S(1)}, u32[]{:S(2)}) copy-start(f32[256]{0:T(256)S(1)} %fusion.104) | copy-start | bytes 3076
  58.2 30.6 %copy-start.41 = (f32[1536]{0:T(1024)}, f32[1536]{0:T(1024)S(1)}, u32[]{:S(2)}) copy-start(f32[1536]{0:T(1024)S(1)} %get-tuple-element.355) | copy-start | bytes 18436
  105.5 82.6 %all-gather.10.cloned.1.call-start = ((), (), s32[]{:S(2)}) async-start(), calls=%async_computation.7 | async-start | bytes 4866048 | tf_op jit(solution)/shard_map/all_gather | solution.py:121
  107.2 381.6 %all-gather.12.cloned.1.call-start = ((), (), s32[]{:S(2)}) async-start(), calls=%async_computation.8 | async-start | bytes 56770560 | tf_op jit(solution)/shard_map/all_gather | solution.py:172
  108.7 547.6 %all-gather.14.cloned.1.call-start = ((), (), s32[]{:S(2)}) async-start(), calls=%async_computation.9 | async-start | bytes 28385280 | tf_op jit(solution)/shard_map/all_gather | solution.py:173
  111.4 662.2 %reduce-scatter.8.cloned.1.call-start = ((), (), s32[]{:S(2)}) async-start(), calls=%async_computation.10 | async-start | bytes 1310720 | tf_op jit(solution)/shard_map/reduce_scatter | solution.py:235
  134.3 53.8 %copy-start.13 = (bf16[2,256,6,128]{1,3,2,0:T(8,128)(2,1)}, bf16[2,256,6,128]{1,3,2,0:T(8,128)(2,1)S(1)}, u32[]{:S(2)}) copy-start(bf16[2,256,6,128]{1,3,2,0:T(8,128)(2,1)S(1)} %get-tuple-element.111) | copy-start | bytes 2359300
  134.3 53.8 %copy-start.17 = (bf16[2,1024,128]{2,1,0:T(8,128)(2,1)}, bf16[2,1024,128]{2,1,0:T(8,128)(2,1)S(1)}, u32[]{:S(2)}) copy-start(bf16[2,1024,128]{2,1,0:T(8,128)(2,1)S(1)} %get-tuple-element.576) | copy-start | bytes 1572868
  750.4 167.3 %reduce-scatter.12.cloned.1.call-start = ((), (), s32[]{:S(2)}) async-start(), calls=%async_computation.12 | async-start | bytes 9732096 | tf_op jit(solution)/shard_map/reduce_scatter | solution.py:258
  756.7 320.9 %reduce-scatter.10.cloned.1.call-start = ((), (), s32[]{:S(2)}) async-start(), calls=%async_computation.11 | async-start | bytes 12976128 | tf_op jit(solution)/shard_map/reduce_scatter | solution.py:257
  785.1 761.5 %reduce-scatter.16.cloned.1.call-start = ((), (), s32[]{:S(2)}) async-start(), calls=%async_computation.14 | async-start | bytes 56770560
  810.2 1627.9 %reduce-scatter.14.cloned.1.call-start = ((), (), s32[]{:S(2)}) async-start(), calls=%async_computation.13 | async-start | bytes 113541120 | tf_op jit(solution)/shard_map/reduce_scatter | solution.py:186
  853.9 1630.6 %copy-start.50 = (s32[160]{0:T(256)}, s32[160]{0:T(256)S(1)}, u32[]{:S(2)}) copy-start(s32[160]{0:T(256)S(1)} %fusion.103) | copy-start | bytes 1924
  875.7 1567.9 %copy-start.46 = (f32[256]{0:T(256)S(1)}, f32[256]{0:T(256)}, u32[]{:S(2)}) copy-start(f32[256]{0:T(256)} %copy-done.45) | copy-start | bytes 3076
  875.7 1608.2 %copy-start.48 = (f32[160]{0:T(256)S(1)}, f32[160]{0:T(256)}, u32[]{:S(2)}) copy-start(f32[160]{0:T(256)} %param.29) | copy-start | bytes 1924
  875.7 1608.2 %copy-start.54 = (f32[160]{0:T(256)S(1)}, f32[160]{0:T(256)}, u32[]{:S(2)}) copy-start(f32[160]{0:T(256)} %param.34) | copy-start | bytes 1924
  875.7 1608.2 %copy-start.55 = (f32[160]{0:T(256)S(1)}, f32[160]{0:T(256)}, u32[]{:S(2)}) copy-start(f32[160]{0:T(256)} %param.39) | copy-start | bytes 1924
  2500.9 45.2 %copy-start.51 = (s32[160]{0:T(256)S(1)}, s32[160]{0:T(256)}, u32[]{:S(2)}) copy-start(s32[160]{0:T(256)} %copy-done.50) | copy-start | bytes 1924
  2500.9 45.9 %copy-start.49 = (f32[160]{0:T(256)S(1)}, f32[160]{0:T(256)}, u32[]{:S(2)}) copy-start(f32[160]{0:T(256)} %param.29) | copy-start | bytes 1924
  (49 other events, 296.8 us)
Sparse Core Ops, SparseCore 0:
  11.5 72.5 all-gather.5
  105.6 15.2 all-gather.7
  124.4 63.6 all-gather.9
  191.4 297.3 all-gather.11
  492.1 164.1 all-gather.13
  750.5 23.0 reduce-scatter.7
  780.5 136.5 reduce-scatter.11
  923.1 154.3 reduce-scatter.9
  1085.1 461.3 reduce-scatter.15
  1552.8 885.2 reduce-scatter.13
where the time goes:
time: 2580 us; the launch traced here: 2570 us
  waiting for transfers between devices  2050 us (79%)
  matrix products  224 us (9%)
  blocking collectives  164 us (6%)
  other arithmetic  81 us (3%)
  local copies, waits for them, and re-layouts  30.9 us (1%)
    reduce_scatter x1, waiting for transfers between devices, shards(): lax.psum_scatter(contract_rows(normed_two, d_gate_up), ('seq', 'fsdp'), s...  889 us
    unnamed x11, waiting for transfers between devices  466 us
    all_gather x1, waiting for transfers between devices, shards(): lax.all_gather(w_gate_up.astype(jnp.bfloat16), ('seq', 'fsdp'), axis=0, t...  296 us
    reduce_scatter x1, waiting for transfers between devices, shards(): lax.psum_scatter(grad_qkv_term, ('seq', 'fsdp'), scatter_dimension=0, til...  158 us
    all_gather x1, waiting for transfers between devices, shards(): lax.all_gather(w_down.astype(jnp.bfloat16), ('seq', 'fsdp'), axis=0, tile...  138 us
    unnamed x2, blocking collectives  83.7 us
    dot_general x4, matrix products, contract_rows(): lax.dot_general(left, right, (((0,), (0,)), ((), ())), preferred_element_...  81 us
    dot_general x4, matrix products, contract_cols(): lax.dot_general(left, right, (((1,), (1,)), ((), ())), preferred_element_...  58.1 us
  transfers between devices with their start and end apart: 10, of which 9 were waited for; matrix products, arithmetic and copies ran while one was open for 7% of the time, Pallas kernels for 0%

commit v1 on v0

--- a/solution.py
+++ b/solution.py
@@ -1,10 +1,13 @@
 from functools import partial
+import itertools
 import math
 
 import jax
 import jax.numpy as jnp
 from jax import lax
-from jax.sharding import PartitionSpec as P
+from jax.experimental import pallas as pl
+from jax.experimental.pallas import tpu as pltpu
+from jax.sharding import Mesh, PartitionSpec as P
 
 D = 1536
 HEADS = 12
@@ -90,6 +93,374 @@
 def spread_trust(trust, labels):
     onehot = labels[:, None] == jnp.arange(piece_count)[None, :]
     return jnp.sum(jnp.where(onehot, trust[None, :], 0.0), axis=1)
+
+
+EVERY = ("x", "core", "z", "y")
+KEEPERS = ("x", "core", "y")
+LINKED = pl.DeviceIdType.MESH
+
+
+def place_of(axes):
+    index = 0
+    for axis in axes:
+        index = index * lax.axis_size(axis) + lax.axis_index(axis)
+    return index
+
+
+def partner(axes, offset):
+    where, index = {}, 0
+    for axis, step in zip(axes, offset):
+        size = lax.axis_size(axis)
+        at = lax.rem(lax.axis_index(axis) + step, size)
+        where[axis] = at
+        index = index * size + at
+    return where, index
+
+
+def hello(partners):
+    barrier = pltpu.get_barrier_semaphore()
+    for where in partners:
+        pl.semaphore_signal(barrier, inc=1, device_id=where, device_id_type=LINKED)
+    pl.semaphore_wait(barrier, len(partners))
+
+
+def push(source, target, send, recv, where):
+    copy = pltpu.make_async_remote_copy(
+        src_ref=source,
+        dst_ref=target,
+        send_sem=send,
+        recv_sem=recv,
+        device_id=where,
+        device_id_type=LINKED,
+    )
+    copy.start()
+    return copy
+
+
+def every_offset(axes):
+    return [o for o in itertools.product(*[range(lax.axis_size(a)) for a in axes]) if any(o)]
+
+
+def exchange_kernel(axes, offsets, cuts, *refs):
+    n = len(cuts)
+    sources, targets, (send_sem, recv_sem, own_sem) = refs[:n], refs[n : 2 * n], refs[2 * n :]
+    me = place_of(axes)
+    partners = [partner(axes, offset) for offset in offsets]
+    owns = []
+    for a in range(n):
+        own = pltpu.make_async_copy(
+            sources[a].at[me] if cuts[a] else sources[a], targets[a].at[me], own_sem.at[a]
+        )
+        own.start()
+        owns.append(own)
+    hello([where for where, _ in partners])
+    copies = []
+    for k, (where, index) in enumerate(partners):
+        for a in range(n):
+            copies.append(
+                push(
+                    sources[a].at[index] if cuts[a] else sources[a],
+                    targets[a].at[me],
+                    send_sem.at[a, k],
+                    recv_sem.at[a, k],
+                    where,
+                )
+            )
+    for copy in owns + copies:
+        copy.wait()
+
+
+def exchange(values, axes, cuts, number, space=pl.ANY):
+    offsets = every_offset(axes)
+    count, n = len(offsets), len(values)
+    return pl.pallas_call(
+        partial(exchange_kernel, axes, offsets, cuts),
+        out_shape=[
+            jax.ShapeDtypeStruct(v.shape if cut else (count + 1,) + v.shape, v.dtype)
+            for v, cut in zip(values, cuts)
+        ],
+        in_specs=[pl.BlockSpec(memory_space=space)] * n,
+        out_specs=[pl.BlockSpec(memory_space=space)] * n,
+        scratch_shapes=[
+            pltpu.SemaphoreType.DMA((n, count)),
+            pltpu.SemaphoreType.DMA((n, count)),
+            pltpu.SemaphoreType.DMA((n,)),
+        ],
+        compiler_params=pltpu.CompilerParams(collective_id=number, has_side_effects=True),
+    )(*values)
+
+
+def spread_kernel(n, m, *refs):
+    sources, rest = refs[: n + m], refs[n + m :]
+    targets, (send_sem, recv_sem, cut_send, cut_recv, own_sem) = rest[: n + m], rest[n + m :]
+    deep = lax.axis_size("z")
+    x, core, z, y = [lax.axis_index(a) for a in EVERY]
+    me = place_of(EVERY)
+    offsets = every_offset(EVERY)
+    partners = [partner(EVERY, offset) for offset in offsets]
+    owns = []
+    for a in range(n + m):
+        own = pltpu.make_async_copy(
+            sources[a] if a < n else sources[a].at[me],
+            targets[a].at[x, core, z, y] if a < n else targets[a].at[me],
+            own_sem.at[a],
+        )
+        own.start()
+        owns.append(own)
+    hello([where for where, _ in partners])
+
+    def owner(dx, dc, dz, dy):
+        return (lax.rem(x + dx, 2), lax.rem(core + dc, 2), lax.rem(z + dz, deep), lax.rem(y + dy, 2))
+
+    def slot(dx, dc, dz, dy):
+        return ((dx * 2 + dc) * deep + dz) * 2 + dy
+
+    pending = []
+
+    def forward(block, axis, step):
+        there = dict(zip(("x", "core", "z", "y"), block))
+        size = lax.axis_size(axis)
+        there[axis] = (there[axis] - step) % size
+        k = slot(*[there[a] for a in EVERY])
+        where = {axis: lax.rem(lax.axis_index(axis) + step, size)}
+        at = owner(*block)
+        for a in range(n):
+            held = sources[a] if not any(block) else targets[a].at[at]
+            pending.append(push(held, targets[a].at[at], send_sem.at[a, k], recv_sem.at[a, k], where))
+
+    def arrived(block):
+        k = slot(*block)
+        at = owner(*block)
+        for a in range(n):
+            pltpu.make_async_remote_copy(
+                src_ref=sources[a],
+                dst_ref=targets[a].at[at],
+                send_sem=send_sem.at[a, k],
+                recv_sem=recv_sem.at[a, k],
+                device_id={"core": lax.rem(core + 1, 2)},
+                device_id_type=LINKED,
+            ).wait_recv()
+
+    own_block = (0, 0, 0, 0)
+    forward(own_block, "x", 1)
+    forward(own_block, "y", 1)
+    for step in range(1, deep):
+        forward(own_block, "z", step)
+    forward(own_block, "core", 1)
+    cut_copies = []
+    for k, (where, index) in enumerate(partners):
+        for a in range(m):
+            cut_copies.append(
+                push(
+                    sources[n + a].at[index],
+                    targets[n + a].at[me],
+                    cut_send.at[a, k],
+                    cut_recv.at[a, k],
+                    where,
+                )
+            )
+    for dz in range(deep):
+        if dz > 0:
+            arrived((0, 0, dz, 0))
+            forward((0, 0, dz, 0), "x", 1)
+            forward((0, 0, dz, 0), "y", 1)
+            forward((0, 0, dz, 0), "core", 1)
+        for block, axis, parity in (((1, 0, dz, 0), "y", 1), ((0, 0, dz, 1), "x", 0)):
+            arrived(block)
+            if dz % 2 == parity:
+                forward(block, axis, 1)
+            forward(block, "core", 1)
+    for dz in range(deep):
+        arrived((1, 0, dz, 1))
+        forward((1, 0, dz, 1), "core", 1)
+    for dx in range(2):
+        for dz in range(deep):
+            for dy in range(2):
+                arrived((dx, 1, dz, dy))
+    for copy in pending:
+        copy.wait_send()
+    for copy in owns + cut_copies:
+        copy.wait()
+
+
+def spread(values, cut_values, number):
+    n, m = len(values), len(cut_values)
+    sizes = tuple(lax.axis_size(a) for a in EVERY)
+    count = math.prod(sizes)
+    if sizes[:2] != (2, 2) or sizes[3] != 2:
+        return [lax.all_gather(v, EVERY, axis=0, tiled=True) for v in values] + list(
+            exchange(cut_values, EVERY, [True] * m, number)
+        )
+    outs = pl.pallas_call(
+        partial(spread_kernel, n, m),
+        out_shape=[jax.ShapeDtypeStruct(sizes + v.shape, v.dtype) for v in values]
+        + [jax.ShapeDtypeStruct(v.shape, v.dtype) for v in cut_values],
+        in_specs=[pl.BlockSpec(memory_space=pl.ANY)] * (n + m),
+        out_specs=[pl.BlockSpec(memory_space=pl.ANY)] * (n + m),
+        scratch_shapes=[
+            pltpu.SemaphoreType.DMA((n, count)),
+            pltpu.SemaphoreType.DMA((n, count)),
+            pltpu.SemaphoreType.DMA((m, count)),
+            pltpu.SemaphoreType.DMA((m, count)),
+            pltpu.SemaphoreType.DMA((n + m,)),
+        ],
+        compiler_params=pltpu.CompilerParams(collective_id=number, has_side_effects=True),
+    )(*values, *cut_values)
+    return [o.reshape((-1,) + v.shape[1:]) for o, v in zip(outs, values)] + list(outs[n:])
+
+
+def add_blocks(count, first, second, store):
+    def step(i, carry):
+        store(i, (first(i).astype(jnp.float32) + second(i).astype(jnp.float32)).astype(jnp.bfloat16))
+        return carry
+
+    lax.fori_loop(0, count, step, 0)
+
+
+def collect_kernel(pieces, width, *refs):
+    n = max(a for a, _ in pieces) + 1
+    sources, targets, scratch = refs[:n], refs[n : 2 * n], refs[2 * n :]
+    r1, a1, r2, a2, r3, a3, r4, send_sem, recv_sem = scratch
+    x, core, z, y = [lax.axis_index(a) for a in EVERY]
+    deep = lax.axis_size("z")
+    half = deep // 2
+    other = {a: {a: lax.rem(lax.axis_index(a) + 1, 2)} for a in ("x", "core", "y")}
+    zs = [{"z": lax.rem(z + k, deep)} for k in range(1, deep)]
+    hello([other["core"], other["x"], other["y"]] + zs)
+    total = len(pieces)
+    going = [{} for _ in pieces]
+
+    def window(p):
+        a, k = pieces[p]
+        return sources[a], pl.ds(k * width, width)
+
+    def go(p, name, s, source, target, where):
+        going[p][name] = push(source, target, send_sem.at[p, s], recv_sem.at[p, s], where)
+
+    def stage(p, s):
+        source, cols = window(p)
+        if s == 1:
+            go(p, "c", 0, source.at[:, 1 - core, :, :, :, cols], r1.at[p], other["core"])
+        if s == 2:
+            going[p]["c"].wait()
+            for i in range(2):
+                for k in range(deep):
+                    def put(t, v, i=i, k=k):
+                        a1[p, i, k, t] = v
+                    add_blocks(
+                        2,
+                        lambda t, i=i, k=k: source[i, core, k, t, :, cols],
+                        lambda t, i=i, k=k: r1[p, i, k, t],
+                        put,
+                    )
+            go(p, "x", 1, a1.at[p, 1 - x, pl.ds(0, half)], r2.at[p, 0], other["x"])
+            go(p, "y", 2, a1.at[p, :, pl.ds(half, half), 1 - y], r2.at[p, 1], other["y"])
+        if s == 3:
+            going[p]["x"].wait()
+            going[p]["y"].wait()
+            for k in range(half):
+                def put_x(t, v, k=k):
+                    a2[p, 0, k, t] = v
+                add_blocks(
+                    2, lambda t, k=k: a1[p, x, k, t], lambda t, k=k: r2[p, 0, k, t], put_x
+                )
+                def put_y(t, v, k=k):
+                    a2[p, 1, t, k] = v
+                add_blocks(
+                    2, lambda t, k=k: a1[p, t, half + k, y], lambda t, k=k: r2[p, 1, t, k], put_y
+                )
+            go(p, "y2", 3, a2.at[p, 0, :, 1 - y], r3.at[p, 0], other["y"])
+            go(p, "x2", 4, a2.at[p, 1, 1 - x], r3.at[p, 1], other["x"])
+        if s == 4:
+            going[p]["y2"].wait()
+            going[p]["x2"].wait()
+            def put_low(t, v):
+                a3[p, t] = v
+            add_blocks(half, lambda t: a2[p, 0, t, y], lambda t: r3[p, 0, t], put_low)
+            def put_high(t, v):
+                a3[p, half + t] = v
+            add_blocks(half, lambda t: a2[p, 1, x, t], lambda t: r3[p, 1, t], put_high)
+            for k in range(1, deep):
+                go(p, k, 4 + k, a3.at[p, lax.rem(z + k, deep)], r4.at[p, k - 1], zs[k - 1])
+        if s == 5:
+            whole = a3[p, z].astype(jnp.float32)
+            for k in range(1, deep):
+                going[p][k].wait()
+                whole = whole + r4[p, k - 1].astype(jnp.float32)
+            a, _ = pieces[p]
+            targets[a][:, cols] = whole
+
+    for t in range(1, total + 5):
+        for s in (5, 4, 3, 2, 1):
+            p = t - s
+            if 0 <= p < total:
+                stage(p, s)
+
+
+def collect(values, number, width=512):
+    sizes = tuple(lax.axis_size(a) for a in EVERY)
+    if sizes[:2] != (2, 2) or sizes[3] != 2 or sizes[2] % 2:
+        return [
+            lax.psum_scatter(v, EVERY, scatter_dimension=0, tiled=True).astype(jnp.float32)
+            for v in values
+        ]
+    rows = values[0].shape[0] // math.prod(sizes)
+    deep = sizes[2]
+    pieces = [(a, k) for a, v in enumerate(values) for k in range(v.shape[1] // width)]
+    total = len(pieces)
+    block = (rows, width)
+    return pl.pallas_call(
+        partial(collect_kernel, pieces, width),
+        out_shape=[jax.ShapeDtypeStruct((rows, v.shape[1]), jnp.float32) for v in values],
+        in_specs=[pl.BlockSpec(memory_space=pltpu.VMEM)] * len(values),
+        out_specs=[pl.BlockSpec(memory_space=pltpu.VMEM)] * len(values),
+        scratch_shapes=[
+            pltpu.VMEM((total, 2, deep, 2) + block, jnp.bfloat16),
+            pltpu.VMEM((total, 2, deep, 2) + block, jnp.bfloat16),
+            pltpu.VMEM((total, 2, deep // 2, 2) + block, jnp.bfloat16)
+            if deep == 4
+            else pltpu.VMEM((total, 2, deep // 2, 2) + block, jnp.bfloat16),
+            pltpu.VMEM((total, 2, deep // 2, 2) + block, jnp.bfloat16),
+            pltpu.VMEM((total, 2, deep // 2) + block, jnp.bfloat16),
+            pltpu.VMEM((total, deep) + block, jnp.bfloat16),
+            pltpu.VMEM((total, deep - 1) + block, jnp.bfloat16),
+            pltpu.SemaphoreType.DMA((total, 4 + deep)),
+            pltpu.SemaphoreType.DMA((total, 4 + deep)),
+        ],
+        compiler_params=pltpu.CompilerParams(
+            collective_id=number, has_side_effects=True, vmem_limit_bytes=56 * 2**20
+        ),
+    )(*[v.reshape(sizes + (rows, v.shape[1])) for v in values])
+
+
+def as_tiles(values):
+    width = -(-values.shape[-1] // 1024) * 1024
+    padded = jnp.pad(values, [(0, 0)] * (values.ndim - 1) + [(0, width - values.shape[-1])])
+    return padded.reshape(values.shape[:-1] + (width // 128, 128))
+
+
+def z_turn(values, step):
+    size = lax.axis_size("z")
+    return lax.ppermute(values, "z", [(i, (i + step) % size) for i in range(size)])
+
+
+def z_ring(values):
+    blocks = [values]
+    for _ in range(lax.axis_size("z") - 1):
+        blocks.append(z_turn(blocks[-1], 1))
+    return jnp.concatenate(blocks, axis=0)
+
+
+def z_return(values):
+    size = lax.axis_size("z")
+    blocks = jnp.split(values, size, axis=0)
+    parts = [blocks[0]] + [z_turn(blocks[k], -k) for k in range(1, size)]
+    return sum(part.astype(jnp.float32) for part in parts)
+
+
+def tiny_gather(values, number):
+    every = exchange([as_tiles(values)], EVERY, [False], number, pltpu.VMEM)[0]
+    return every.reshape(every.shape[0], -1)[:, : values.shape[0]]
 
 
 def shards(
@@ -116,19 +487,33 @@
     kv_width = KV_HEADS * HEAD_DIM
     group = HEADS // KV_HEADS
     score_scale = 1.0 / math.sqrt(HEAD_DIM)
-    qkv_full, out_full, small_full = (
-        lax.all_gather(w_qkv.astype(jnp.bfloat16), ("seq", "fsdp"), axis=0, tiled=True),
-        lax.all_gather(w_out.astype(jnp.bfloat16), ("seq", "fsdp"), axis=0, tiled=True),
-        lax.all_gather(small_params.astype(jnp.bfloat16), ("seq", "fsdp"), axis=0, tiled=True),
-    )
-    small_wide = small_full.astype(jnp.float32)
+    devices = math.prod(lax.axis_size(axis) for axis in EVERY)
+    units = FF // devices
+    rows_d = D // devices
+    wide = -(-2 * units // 128) * 128
+    small_wide = tiny_gather(
+        small_params.astype(jnp.bfloat16).astype(jnp.float32), 0
+    ).reshape(-1)
+    cut = w_gate_up.astype(jnp.bfloat16).reshape(rows_d, 2, devices, units).transpose(2, 0, 1, 3)
+    cut = jnp.pad(cut.reshape(devices, rows_d, 2 * units), ((0, 0), (0, 0), (0, wide - 2 * units)))
+    qkv_full, out_full, traded = spread(
+        [w_qkv.astype(jnp.bfloat16), w_out.astype(jnp.bfloat16)], [cut], 1
+    )
+    own_gate_up = traded.reshape(D, wide)[:, : 2 * units].T
+    own_units = jnp.concatenate([own_gate_up, w_down.astype(jnp.bfloat16)], axis=0)
+    unit_rows = lax.all_gather(own_units, KEEPERS, axis=0)
+    gate_full = unit_rows[:, :units].reshape(-1, D)
+    up_full = unit_rows[:, units : 2 * units].reshape(-1, D)
+    down_full = unit_rows[:, 2 * units :].reshape(-1, D)
+    cot_low = cotangent[0]
+    cot_group = z_ring(cot_low)
     bias = small_wide[:QKV]
     gain_one = small_wide[QKV : QKV + D]
     gain_two = small_wide[QKV + D :]
     inputs = tokens[0].astype(jnp.float32)
     rows = inputs.shape[0]
-    length = rows * lax.axis_size("seq")
-    places = lax.axis_index("seq") * rows + jnp.arange(rows)
+    length = rows * (lax.axis_size("x") * lax.axis_size("core"))
+    places = place_of(("x", "core")) * rows + jnp.arange(rows)
     key_places = jnp.arange(length)
     starts = doc_starts(doc_lengths[0], places)
     allowed = (key_places[None, :] <= places[:, None]) & (key_places[None, :] >= starts[:, None])
@@ -140,9 +525,9 @@
     value_low = projected[:, heads_width + kv_width :].astype(jnp.bfloat16)
     query_low = rope_turn(query_raw, cosine, sine).astype(jnp.bfloat16)
     key_low = rope_turn(key_raw, cosine, sine).astype(jnp.bfloat16).reshape(rows, kv_width)
-    kv_rows = lax.all_gather(
-        jnp.concatenate([key_low, value_low], axis=1), "seq", axis=0, tiled=True
-    )
+    kv_rows = exchange(
+        [jnp.concatenate([key_low, value_low], axis=1)], ("x", "core"), [False], 2
+    )[0].reshape(length, 2 * kv_width)
     keys_grouped = kv_rows[:, :kv_width].reshape(length, KV_HEADS, HEAD_DIM).transpose(1, 0, 2)
     values_grouped = kv_rows[:, kv_width:].reshape(length, KV_HEADS, HEAD_DIM).transpose(1, 0, 2)
     query_grouped = query_low.reshape(rows, KV_HEADS, group, HEAD_DIM).transpose(1, 0, 2, 3)
@@ -167,24 +552,40 @@
     mixed_low = mixed.transpose(1, 0, 2, 3).reshape(rows, heads_width).astype(jnp.bfloat16)
     middle = inputs + jnp.dot(mixed_low, out_full, preferred_element_type=jnp.float32)
     normed_two = normed(middle, gain_two).astype(jnp.bfloat16)
-    cot_low = cotangent[0]
-    gate_up_full, down_full = (
-        lax.all_gather(w_gate_up.astype(jnp.bfloat16), ("seq", "fsdp"), axis=0, tiled=True),
-        lax.all_gather(w_down.astype(jnp.bfloat16), ("seq", "fsdp"), axis=0, tiled=True),
-    )
-    gate_up = jnp.dot(normed_two, gate_up_full, preferred_element_type=jnp.float32)
-    hidden, swish_back = jax.vjp(swish_product, gate_up[:, :FF], gate_up[:, FF:])
+    group_two = z_ring(normed_two)
+    gate = contract_cols(group_two, gate_full)
+    upper = contract_cols(group_two, up_full)
+    hidden, swish_back = jax.vjp(swish_product, gate, upper)
     hidden_low = hidden.astype(jnp.bfloat16)
-    mlp_term = jnp.dot(hidden_low, down_full, preferred_element_type=jnp.float32)
-    d_hidden = contract_cols(cot_low, down_full)
+    d_hidden = contract_cols(cot_group, down_full)
     d_gate, d_upper = swish_back(d_hidden)
-    d_gate_up = jnp.concatenate([d_gate, d_upper], axis=1).astype(jnp.bfloat16)
-    d_normed_two = contract_cols(d_gate_up, gate_up_full)
-    grad_down = lax.psum_scatter(
-        contract_rows(hidden_low, cot_low), ("seq", "fsdp"), scatter_dimension=0, tiled=True
-    )
-    grad_gate_up = lax.psum_scatter(
-        contract_rows(normed_two, d_gate_up), ("seq", "fsdp"), scatter_dimension=0, tiled=True
+    d_gate = d_gate.astype(jnp.bfloat16)
+    d_upper = d_upper.astype(jnp.bfloat16)
+    d_two_part = jnp.dot(d_gate, gate_full, preferred_element_type=jnp.float32) + jnp.dot(
+        d_upper, up_full, preferred_element_type=jnp.float32
+    )
+    zs = lax.axis_size("z")
+    d_normed_two = z_return(d_two_part.astype(jnp.bfloat16))
+    mlp_part = jnp.dot(hidden_low, down_full, preferred_element_type=jnp.float32)
+    mlp_term = z_return(mlp_part.astype(jnp.bfloat16))
+    keepers = devices // zs
+    unit_grads = jnp.concatenate(
+        [
+            contract_rows(a, b).astype(jnp.bfloat16).reshape(keepers, units, D)
+            for a, b in ((d_gate, group_two), (d_upper, group_two), (hidden_low, cot_group))
+        ],
+        axis=1,
+    )
+    own_grads = lax.psum_scatter(unit_grads, KEEPERS, scatter_dimension=0, tiled=False)
+    grad_down = own_grads[2 * units :].astype(jnp.float32)
+    back = jnp.pad(own_grads[: 2 * units].T, ((0, 0), (0, wide - 2 * units)))
+    back = exchange([back.reshape(devices, rows_d, wide)], EVERY, [True], 6)[0]
+    grad_gate_up = (
+        back[:, :, : 2 * units]
+        .reshape(devices, rows_d, 2, units)
+        .transpose(1, 2, 0, 3)
+        .reshape(rows_d, 2 * FF)
+        .astype(jnp.float32)
     )
     block_out = (middle + mlp_term).astype(jnp.bfloat16)[None]
     unused_two, norm_two_back = jax.vjp(normed, middle, gain_two)
@@ -232,9 +633,10 @@
         ],
         axis=1,
     )
-    d_kv_local = lax.psum_scatter(
-        d_kv_rows.astype(jnp.bfloat16), "seq", scatter_dimension=0, tiled=True
-    ).astype(jnp.float32)
+    d_kv_every = exchange(
+        [d_kv_rows.astype(jnp.bfloat16).reshape(-1, rows, 2 * kv_width)], ("x", "core"), [True], 3
+    )[0]
+    d_kv_local = jnp.sum(d_kv_every.astype(jnp.float32), axis=0)
     unused_query, rope_query_back = jax.vjp(partial(rope_turn, cosine=cosine, sine=sine), query_raw)
     unused_key, rope_key_back = jax.vjp(partial(rope_turn, cosine=cosine, sine=sine), key_raw)
     (d_query_raw,) = rope_query_back(d_query.transpose(1, 0, 2, 3).reshape(rows, HEADS, HEAD_DIM))
@@ -253,21 +655,17 @@
     unused_one, norm_one_back = jax.vjp(normed, inputs, gain_one)
     d_inputs, d_gain_one = norm_one_back(d_normed_one)
     tokens_grad = (d_middle + d_inputs).astype(jnp.bfloat16)[None]
-    grad_qkv, grad_out, grad_small = (
-        lax.psum_scatter(grad_qkv_term, ("seq", "fsdp"), scatter_dimension=0, tiled=True),
-        lax.psum_scatter(grad_out_term, ("seq", "fsdp"), scatter_dimension=0, tiled=True),
-        lax.psum_scatter(
-            jnp.concatenate([d_bias, d_gain_one, d_gain_two]),
-            ("seq", "fsdp"),
-            scatter_dimension=0,
-            tiled=True,
-        ),
-    )
+    grad_out, grad_qkv = collect(
+        [grad_out_term.astype(jnp.bfloat16), grad_qkv_term.astype(jnp.bfloat16)], 4
+    )
+    small_terms = jnp.concatenate([d_bias, d_gain_one, d_gain_two]).reshape(devices, -1)
+    small_every = exchange([as_tiles(small_terms)], EVERY, [True], 5, pltpu.VMEM)[0]
+    grad_small = jnp.sum(small_every, axis=0).reshape(-1)[: small_terms.shape[1]]
     masters = (w_qkv, w_out, w_gate_up, w_down, small_params)
     grads = (grad_qkv, grad_out, grad_gate_up, grad_down, grad_small)
     firsts = (first_qkv, first_out, first_gate_up, first_down, first_small)
     seconds = (second_qkv, second_out, second_gate_up, second_down, second_small)
-    small_offset = lax.axis_index(("seq", "fsdp")) * small_params.shape[0]
+    small_offset = place_of(EVERY) * small_params.shape[0]
     labels = (
         part_labels(QKV, [heads_width, heads_width + kv_width], 0, 0),
         part_labels(D, [], 3, 0),
@@ -287,7 +685,8 @@
         ),
         axis=0,
     )
-    grad_total, weight_total = lax.psum((grad_local, weight_local), ("seq", "fsdp"))
+    totals = jnp.sum(tiny_gather(jnp.concatenate([weight_local, grad_local[None]]), 7), axis=0)
+    weight_total, grad_total = totals[:piece_count], totals[piece_count]
     grad_norm = jnp.sqrt(grad_total)
     factor = jnp.minimum(1.0, math.sqrt(NPARAMS) / grad_norm)
     results = []
@@ -308,7 +707,7 @@
         ),
         axis=0,
     )
-    update_total = lax.psum(update_local, ("seq", "fsdp"))
+    update_total = jnp.sum(tiny_gather(update_local, 8), axis=0)
     weight_norm = jnp.sqrt(weight_total)
     update_norm = jnp.sqrt(update_total)
     trust = weight_norm / (update_norm + trust_eps)
@@ -341,49 +740,52 @@
 
 
 def solution(mesh):
+    seq, fsdp = mesh.shape["seq"], mesh.shape["fsdp"]
+    deep = 4 if fsdp % 4 == 0 else 1
+    mesh = Mesh(mesh.devices.reshape(seq // 2, 2, deep, fsdp // deep), EVERY)
     return jax.shard_map(
         shards,
         mesh=mesh,
         in_specs=(
-            P("fsdp", "seq", None),
-            P("fsdp", "seq", None),
-            P("fsdp", None),
-            P(("seq", "fsdp"), None),
-            P(("seq", "fsdp"), None),
-            P(("seq", "fsdp"), None),
-            P(("seq", "fsdp"), None),
-            P(("seq", "fsdp")),
-            P(("seq", "fsdp"), None),
-            P(("seq", "fsdp"), None),
-            P(("seq", "fsdp"), None),
-            P(("seq", "fsdp"), None),
-            P(("seq", "fsdp")),
-            P(("seq", "fsdp"), None),
-            P(("seq", "fsdp"), None),
-            P(("seq", "fsdp"), None),
-            P(("seq", "fsdp"), None),
-            P(("seq", "fsdp")),
+            P(("z", "y"), ("x", "core"), None),
+            P(("z", "y"), ("x", "core"), None),
+            P(("z", "y"), None),
+            P(EVERY, None),
+            P(EVERY, None),
+            P(EVERY, None),
+            P(EVERY, None),
+            P(EVERY),
+            P(EVERY, None),
+            P(EVERY, None),
+            P(EVERY, None),
+            P(EVERY, None),
+            P(EVERY),
+            P(EVERY, None),
+            P(EVERY, None),
+            P(EVERY, None),
+            P(EVERY, None),
+            P(EVERY),
         ),
         out_specs=(
-            P("fsdp", "seq", None),
-            P("fsdp", "seq", None),
+            P(("z", "y"), ("x", "core"), None),
+            P(("z", "y"), ("x", "core"), None),
             P(),
             P(),
-            P(("seq", "fsdp"), None),
-            P(("seq", "fsdp"), None),
-            P(("seq", "fsdp"), None),
-            P(("seq", "fsdp"), None),
-            P(("seq", "fsdp")),
-            P(("seq", "fsdp"), None),
-            P(("seq", "fsdp"), None),
-            P(("seq", "fsdp"), None),
-            P(("seq", "fsdp"), None),
-            P(("seq", "fsdp")),
-            P(("seq", "fsdp"), None),
-            P(("seq", "fsdp"), None),
-            P(("seq", "fsdp"), None),
-            P(("seq", "fsdp"), None),
-            P(("seq", "fsdp")),
+            P(EVERY, None),
+            P(EVERY, None),
+            P(EVERY, None),
+            P(EVERY, None),
+            P(EVERY),
+            P(EVERY, None),
+            P(EVERY, None),
+            P(EVERY, None),
+            P(EVERY, None),
+            P(EVERY),
+            P(EVERY, None),
+            P(EVERY, None),
+            P(EVERY, None),
+            P(EVERY, None),
+            P(EVERY),
         ),
         check_vma=False,
     )

time: 2580 us -> 889 us (0.34)
  waiting for transfers between devices: 2050 us -> 197 us
  Pallas kernels: 0 us -> 313 us
  blocking collectives: 164 us -> 0 us
  matrix products: 224 us -> 154 us
  local copies, waits for them, and re-layouts: 30.9 us -> 85.8 us
    reduce_scatter x4 -> x1, waiting for transfers between devices: 1060 us -> 0.01 us  [shards(): lax.psum_scatter(unit_grads, KEEPERS, scatter_dimension=0, tiled=False)]
    all_gather x5 -> x1, waiting for transfers between devices: 521 us -> 0.02 us  [shards(): unit_rows = lax.all_gather(own_units, KEEPERS, axis=0)]
    unnamed x11 -> x2, waiting for transfers between devices: 466 us -> 0.03 us
    pallas_call x0 -> x9, Pallas kernels: none -> 313 us  [the longest x7 149 us: exchange(): pl.pallas_call(partial(exchange_kernel, axes, offsets, cuts), out_shape=[...]
    ppermute x0 -> x12, waiting for transfers between devices: none -> 197 us  [z_turn(): lax.ppermute(values, 'z', [(i, (i + step) % size) for i in range(size)])]
    unnamed x2 -> x0, blocking collectives: 83.7 us -> none
    psum x2 -> x0, blocking collectives: 79.8 us -> none  [the longest x1 40.2 us: shards(): update_total = lax.psum(update_local, ('seq', 'fsdp'))]
    dot_general x4 -> x5, matrix products: 81 us -> 37.5 us  [contract_rows(): lax.dot_general(left, right, (((0,), (0,)), ((), ())), preferred_element_...]
  transfers between devices with their start and end apart: 10 -> 14, of which waited for: 9 -> 9; matrix products, arithmetic and copies ran while one was open for 7% -> 19% of each run, Pallas kernels for 0% -> 17%
where the time goes in v1:
time: 889 us; the launch traced here: 882 us
  Pallas kernels  313 us (35%)
  waiting for transfers between devices  197 us (22%)
  matrix products  154 us (17%)
  other arithmetic  102 us (11%)
  local copies, waits for them, and re-layouts  85.8 us (10%)
  between operations  21.3 us (2%)
    ppermute x12, waiting for transfers between devices, z_turn(): lax.ppermute(values, 'z', [(i, (i + step) % size) for i in range(size)])  197 us
    pallas_call x7, Pallas kernels, exchange(): pl.pallas_call(partial(exchange_kernel, axes, offsets, cuts), out_shape=[...  149 us
    pallas_call x1, Pallas kernels, spread(): pl.pallas_call(partial(spread_kernel, n, m), out_shape=[jax.ShapeDtypeStr...  94.6 us
    pallas_call x1, Pallas kernels, collect(): pl.pallas_call(partial(collect_kernel, pieces, width), out_shape=[jax.Sha...  68.8 us
    dot_general x5, matrix products, contract_cols(): lax.dot_general(left, right, (((1,), (1,)), ((), ())), preferred_element_...  50.3 us
    dot_general x5, matrix products, contract_rows(): lax.dot_general(left, right, (((0,), (0,)), ((), ())), preferred_element_...  37.5 us
    reduce_sum x8, other arithmetic, column_squares(): return jnp.sum(values * values, axis=0)  23 us
    unnamed x214, local copies, waits for them, and re-layouts  20.7 us
  transfers between devices with their start and end apart: 14, of which 9 were waited for; matrix products, arithmetic and copies ran while one was open for 19% of the time, Pallas kernels for 17%

profile of v1, /device:TPU:0, one launch (start us, length us, event | category | flops | bytes accessed | tf_op | source)
XLA Modules:
  0.0 881.8 jit_solution(12301263682723950412)
XLA Ops:
  30.7 94.6 %shard_map.322 = (bf16[2,2,4,2,48,2048]{5,4,3,2,1,0:T(8,128)(2,1)}, bf16[2,2,4,2,48,1536]{5,4,3,2,1,0:T(8,128)(2,1)}, bf16[32,48,640]{2,1,0:T(8,128)(2,1)}) custom-call(bf16[48,2048]{1,0:T(8,128)(2,1)} %get-tuple-element.318.refs_0_, bf16[48,1536]{1,0:T(8,128)(2,1)} %get-tuple-element.320.refs_1_, bf16[32,48,640]{2,1,0:T(8,128)(2,1)} %pad.38.refs_2_), custom_call_target="tpu_custom_call" | custom-call | tf_op jit(solution)/shard_map/pallas_call | solution.py:294
  133.7 30.9 %shard_map.321 = f32[32,8,128]{2,1,0:T(8,128)} custom-call(f32[8,128]{1,0:T(8,128)} %bitcast_convert_fusion.refs_0_), custom_call_target="tpu_custom_call" | custom-call | tf_op jit(solution)/shard_map/pallas_call | solution.py:176
  177.5 24.5 %shard_map.323 = bf16[4,256,512]{2,1,0:T(8,128)(2,1)} custom-call(bf16[256,512]{1,0:T(8,128)(2,1)} %pad_maximum_fusion.8.refs_0_), custom_call_target="tpu_custom_call" | custom-call | tf_op jit(solution)/shard_map/pallas_call | solution.py:176
  214.7 11.7 %while.28 = (s32[]{:T(128)}, bf16[2,256,6,128]{1,3,2,0:T(8,128)(2,1)S(1)}, f32[2,256,6]{1,2,0:T(8,128)}, bf16[2,256,6,128]{3,1,2,0:T(8,128)(2,1)S(1)}, bf16[2,10...) while((s32[]{:T(128)}, ...), condition=%wide.region_6.7_spmd.clone, body=%wide.region_3.6_spmd.clone.sunk | while | flops 824965632 | bytes 21788824 | solution.py:551
  235.2 19.7 %collective-permute-done = bf16[256,1536]{1,0:T(8,128)(2,1)S(1)} collective-permute-done((bf16[256,1536]{1,0:T(8,128)(2,1)S(1)}, bf16[256,1536]{1,0:T(8,128)(2,1)S(1)}, u32[]{:S(2)}, u32[]{:S(2)}) %collective-permute-start) | collective-permute-done | bytes 786464 | tf_op jit(solution)/shard_map/ppermute | solution.py:444
  254.8 16.8 %collective-permute-done.6 = bf16[256,1536]{1,0:T(8,128)(2,1)S(1)} collective-permute-done((bf16[256,1536]{1,0:T(8,128)(2,1)S(1)}, bf16[256,1536]{1,0:T(8,128)(2,1)S(1)}, u32[]{:S(2)}, u32[]{:S(2)}) %collective-permute-start.6) | collective-permute-done | bytes 786464 | tf_op jit(solution)/shard_map/ppermute | solution.py:444
  271.7 16.8 %collective-permute-done.1 = bf16[256,1536]{1,0:T(8,128)(2,1)S(1)} collective-permute-done((bf16[256,1536]{1,0:T(8,128)(2,1)S(1)}, bf16[256,1536]{1,0:T(8,128)(2,1)S(1)}, u32[]{:S(2)}, u32[]{:S(2)}) %collective-permute-start.1) | collective-permute-done | bytes 786464 | tf_op jit(solution)/shard_map/ppermute | solution.py:444
  288.5 17.0 %collective-permute-done.7 = bf16[256,1536]{1,0:T(8,128)(2,1)} collective-permute-done((bf16[256,1536]{1,0:T(8,128)(2,1)S(1)}, bf16[256,1536]{1,0:T(8,128)(2,1)}, u32[]{:S(2)}, u32[]{:S(2)}) %collective-permute-start.7) | collective-permute-done | bytes 786464 | tf_op jit(solution)/shard_map/ppermute | solution.py:444
  322.3 10.8 %fusion.121 = f32[1024,2240]{0,1:T(8,128)} fusion(bf16[2240,1536]{1,0:T(8,128)(2,1)S(1)} %bitcast.309, bf16[256,1536]{1,0:T(8,128)(2,1)} %collective-permute-done.2, bf16[256,1536]{1,0:T(8,128)(2,1)S(1)} %collective-permute-done.1, bf16[256,1536]{1,0:T(8,128)(2,1)S(1)} %collective-permute-done, bf16[256,1536]{1,0:T(8,128)(2,1)S(1)} %multiply_convert_fusion.3), kind=kOutput, calls=%fused_computation.267 | convolution fusion | flops 7059013632 | bytes 19202048 | tf_op jit(solution)/shard_map/dot_general | solution.py:69
  333.1 10.7 %fusion.122 = f32[1024,2240]{0,1:T(8,128)} fusion(bf16[2240,1536]{1,0:T(8,128)(2,1)S(1)} %bitcast.313, bf16[256,1536]{1,0:T(8,128)(2,1)} %collective-permute-done.2, bf16[256,1536]{1,0:T(8,128)(2,1)} %copy-done.96, bf16[256,1536]{1,0:T(8,128)(2,1)S(1)} %collective-permute-done, bf16[256,1536]{1,0:T(8,128)(2,1)S(1)} %multiply_convert_fusion.3), kind=kOutput, calls=%fused_computation.268 | convolution fusion | flops 7059013632 | bytes 19202048 | tf_op jit(solution)/shard_map/dot_general | solution.py:69
  343.8 21.3 %multiply_convert_fusion.1 = (bf16[1024,2240]{0,1:T(8,128)(2,1)}, bf16[1024,2240]{0,1:T(8,128)(2,1)}, bf16[1024,2240]{0,1:T(8,128)(2,1)}) fusion(f32[1024,2240]{0,1:T(8,128)} %fusion.122, f32[1024,2240]{0,1:T(8,128)} %fusion.121, bf16[2240,1536]{1,0:T(8,128)(2,1)} %bitcast.305, bf16[256,1536]{1,0:T(8,128)(2,1)} %collective-permute-done.8, ...), kind=kOutput, calls=%fused_computation.75 | convolution fusion | flops 7095713792 | bytes 42139648 | tf_op jit(solution)/shard_map/dot_general | solution.py:69
  365.2 10.3 %convolution_convert_fusion.2 = bf16[2240,1536]{1,0:T(8,128)(2,1)S(1)} fusion(bf16[1024,2240]{0,1:T(8,128)(2,1)} %get-tuple-element.297, bf16[256,1536]{1,0:T(8,128)(2,1)} %collective-permute-done.2, bf16[256,1536]{1,0:T(8,128)(2,1)} %copy-done.96, bf16[256,1536]{1,0:T(8,128)(2,1)S(1)} %collective-permute-done, bf16[256,1536]{1,0:T(8,128)(2,1)S(1)} %multiply_convert_fusion.3), kind=kOutput, calls=%fused_computation.71 | convolution fusion | flops 7062454272 | bytes 14614528 | tf_op jit(solution)/shard_map/dot_general | solution.py:63
  394.5 17.1 %pad_maximum_fusion = bf16[8,840,1536]{2,1,0:T(8,128)(2,1)} fusion(bf16[8,280,1536]{2,1,0:T(8,128)(2,1)S(1)} %bitcast.317, bf16[8,280,1536]{2,1,0:T(8,128)(2,1)S(1)} %bitcast.316, bf16[8,280,1536]{2,1,0:T(8,128)(2,1)S(1)} %bitcast.315), kind=kLoop, calls=%fused_computation.67 | loop fusion | flops 61931520 | bytes 41287680 | tf_op jit(solution)/shard_map/concatenate | solution.py:572
  416.3 13.7 %fusion.138 = f32[1024,1536]{1,0:T(8,128)S(1)} fusion(bf16[1024,2240]{0,1:T(8,128)(2,1)} %get-tuple-element.297, bf16[2240,1536]{1,0:T(8,128)(2,1)} %bitcast.314), kind=kOutput, calls=%fused_computation.278 | convolution fusion | flops 7046430720 | bytes 17760256 | tf_op jit(solution)/shard_map/dot_general | solution.py:564
  454.1 37.6 %collective-permute-done.10 = bf16[256,1536]{1,0:T(8,128)(2,1)S(1)} collective-permute-done((bf16[256,1536]{1,0:T(8,128)(2,1)S(1)}, bf16[256,1536]{1,0:T(8,128)(2,1)S(1)}, u32[]{:S(2)}, u32[]{:S(2)}) %collective-permute-start.10) | collective-permute-done | bytes 786464 | tf_op jit(solution)/shard_map/ppermute | solution.py:444
  497.1 13.0 %collective-permute-done.3 = bf16[256,1536]{1,0:T(8,128)(2,1)S(1)} collective-permute-done((bf16[256,1536]{1,0:T(8,128)(2,1)S(1)}, bf16[256,1536]{1,0:T(8,128)(2,1)S(1)}, u32[]{:S(2)}, u32[]{:S(2)}) %collective-permute-start.3) | collective-permute-done | bytes 786464 | tf_op jit(solution)/shard_map/ppermute | solution.py:444
  510.1 65.8 %collective-permute-done.4 = bf16[256,1536]{1,0:T(8,128)(2,1)S(1)} collective-permute-done((bf16[256,1536]{1,0:T(8,128)(2,1)S(1)}, bf16[256,1536]{1,0:T(8,128)(2,1)S(1)}, u32[]{:S(2)}, u32[]{:S(2)}) %collective-permute-start.4) | collective-permute-done | bytes 786464 | tf_op jit(solution)/shard_map/ppermute | solution.py:444
  581.1 21.6 %while.29 = (s32[]{:T(128)}, f32[2,256,6,128]{3,1,2,0:T(8,128)}, bf16[2,1024,128]{2,1,0:T(8,128)(2,1)}, bf16[2,1024,128]{2,1,0:T(8,128)(2,1)}, bf16[2,256,6,128]...) while((s32[]{:T(128)}, f32[2,256,6,128]{3,1,2,0:T(8,128)}, ...), condition=%wide.region_11.12_spmd.clone, body=%wide.region_9.11_spmd.clone.sunk | while | flops 2037971456 | bytes 69260520 | solution.py:626
  607.6 14.2 %shard_map.324 = bf16[4,256,512]{2,1,0:T(8,128)(2,1)} custom-call(bf16[4,256,512]{2,1,0:T(8,128)(2,1)} %pad_maximum_fusion.4.refs_0_), custom_call_target="tpu_custom_call" | custom-call | tf_op jit(solution)/shard_map/pallas_call | solution.py:176
  635.2 10.7 %shard_map.327 = f32[32,8,128]{2,1,0:T(8,128)} custom-call(f32[32,8,128]{2,1,0:T(8,128)} %bitcast.336), custom_call_target="tpu_custom_call" | custom-call | tf_op jit(solution)/shard_map/pallas_call | solution.py:176
  655.0 68.8 %shard_map.325 = (f32[48,1536]{1,0:T(8,128)}, f32[48,2048]{1,0:T(8,128)}) custom-call(bf16[2,2,4,2,48,1536]{5,4,3,2,1,0:T(8,128)(2,1)} %bitcast.288, bf16[2,2,4,2,48,2048]{5,4,3,2,1,0:T(8,128)(2,1)} %bitcast.287), custom_call_target="tpu_custom_call" | custom-call | tf_op jit(solution)/shard_map/pallas_call | solution.py:412
  738.8 45.9 %shard_map.326 = bf16[32,48,640]{2,1,0:T(8,128)(2,1)} custom-call(bf16[32,48,640]{2,1,0:T(8,128)(2,1)} %bitcast.301), custom_call_target="tpu_custom_call" | custom-call | tf_op jit(solution)/shard_map/pallas_call | solution.py:176
  792.9 12.9 %shard_map.328 = f32[32,8,128]{2,1,0:T(8,128)} custom-call(f32[8,128]{1,0:T(8,128)} %fusion.109.refs_0_), custom_call_target="tpu_custom_call" | custom-call | tf_op jit(solution)/shard_map/pallas_call | solution.py:176
  848.2 10.3 %shard_map.329 = f32[32,8,128]{2,1,0:T(8,128)} custom-call(f32[8,128]{1,0:T(8,128)} %pad_bitcast_fusion.1.refs_0_), custom_call_target="tpu_custom_call" | custom-call | tf_op jit(solution)/shard_map/pallas_call | solution.py:176
  (426 shorter events, 276.8 us)
Async XLA Ops:
  7.2 298.5 %all-gather.3.cloned.1.call-start = ((), (), s32[]{:S(2)}) async-start(), calls=%async_computation.2 | async-start | bytes 23224320 | tf_op jit(solution)/shard_map/all_gather | solution.py:504
  30.7 98.5 %copy-start.8 = (f32[280,1536]{1,0:T(8,128)S(1)}, f32[280,1536]{1,0:T(8,128)}, u32[]{:S(2)}) copy-start(f32[280,1536]{1,0:T(8,128)} %param.28) | copy-start | bytes 5160964
  132.3 599.6 %reduce-scatter.2.cloned.1.call-start = ((), (), s32[]{:S(2)}) async-start(), calls=%async_computation.1 | async-start | bytes 23224320 | tf_op jit(solution)/shard_map/reduce_scatter | solution.py:579
  166.5 64.8 %copy-start.65 = (f32[1536]{0:T(1024)}, f32[1536]{0:T(1024)S(1)}, u32[]{:S(2)}) copy-start(f32[1536]{0:T(1024)S(1)} %get-tuple-element.327) | copy-start | bytes 18436
  231.2 84.7 %copy-start.80 = (f32[256]{0:T(256)}, f32[256]{0:T(256)S(1)}, u32[]{:S(2)}) copy-start(f32[256]{0:T(256)S(1)} %get-tuple-element.334) | copy-start | bytes 3076
  232.6 22.2 %collective-permute-start = (bf16[256,1536]{1,0:T(8,128)(2,1)S(1)}, bf16[256,1536]{1,0:T(8,128)(2,1)S(1)}, u32[]{:S(2)}, u32[]{:S(2)}) collective-permute-start(bf16[256,1536]{1,0:T(8,128)(2,1)S(1)} %multiply_convert_fusion.3), channel_id=1, source_target_pairs={{0,2},{2,4},{4,6},{6,0},{1,3},{3,5},{5,7},{7,1},{8,10},{10,12},{12... | collective-permute-start | bytes 2359304 | tf_op jit(solution)/shard_map/ppermute | solution.py:444
  234.1 37.6 %collective-permute-start.6 = (bf16[256,1536]{1,0:T(8,128)(2,1)S(1)}, bf16[256,1536]{1,0:T(8,128)(2,1)S(1)}, u32[]{:S(2)}, u32[]{:S(2)}) collective-permute-start(bf16[256,1536]{1,0:T(8,128)(2,1)S(1)} %bitcast.331), channel_id=1, source_target_pairs={{0,2},{2,4},{4,6},{6,0},{1,3},{3,5},{5,7},{7,1},{8,10},{10,12},{12... | collective-permute-start | bytes 2359304 | tf_op jit(solution)/shard_map/ppermute | solution.py:444
  254.8 33.7 %collective-permute-start.1 = (bf16[256,1536]{1,0:T(8,128)(2,1)S(1)}, bf16[256,1536]{1,0:T(8,128)(2,1)S(1)}, u32[]{:S(2)}, u32[]{:S(2)}) collective-permute-start(bf16[256,1536]{1,0:T(8,128)(2,1)S(1)} %collective-permute-done), channel_id=1, source_target_pairs={{0,2},{2,4},{4,6},{6,0},{1,3},{3,5},{5,7},{7,1},{8,10},{10,12},{12... | collective-permute-start | bytes 2359304 | tf_op jit(solution)/shard_map/ppermute | solution.py:444
  271.7 33.8 %collective-permute-start.7 = (bf16[256,1536]{1,0:T(8,128)(2,1)S(1)}, bf16[256,1536]{1,0:T(8,128)(2,1)}, u32[]{:S(2)}, u32[]{:S(2)}) collective-permute-start(bf16[256,1536]{1,0:T(8,128)(2,1)S(1)} %collective-permute-done.6), channel_id=1, source_target_pairs={{0,2},{2,4},{4,6},{6,0},{1,3},{3,5},{5,7},{7,1},{8,10},{10,12},{12... | collective-permute-start | bytes 2359304 | tf_op jit(solution)/shard_map/ppermute | solution.py:444
  288.5 33.8 %collective-permute-start.2 = (bf16[256,1536]{1,0:T(8,128)(2,1)S(1)}, bf16[256,1536]{1,0:T(8,128)(2,1)}, u32[]{:S(2)}, u32[]{:S(2)}) collective-permute-start(bf16[256,1536]{1,0:T(8,128)(2,1)S(1)} %collective-permute-done.1), channel_id=1, source_target_pairs={{0,2},{2,4},{4,6},{6,0},{1,3},{3,5},{5,7},{7,1},{8,10},{10,12},{12... | collective-permute-start | bytes 2359304 | tf_op jit(solution)/shard_map/ppermute | solution.py:444
  305.5 38.3 %collective-permute-start.8 = (bf16[256,1536]{1,0:T(8,128)(2,1)}, bf16[256,1536]{1,0:T(8,128)(2,1)}, u32[]{:S(2)}, u32[]{:S(2)}) collective-permute-start(bf16[256,1536]{1,0:T(8,128)(2,1)} %collective-permute-done.7), channel_id=1, source_target_pairs={{0,2},{2,4},{4,6},{6,0},{1,3},{3,5},{5,7},{7,1},{8,10},{10,12},{12... | collective-permute-start | bytes 2359304 | tf_op jit(solution)/shard_map/ppermute | solution.py:444
  440.5 51.2 %collective-permute-start.10 = (bf16[256,1536]{1,0:T(8,128)(2,1)S(1)}, bf16[256,1536]{1,0:T(8,128)(2,1)S(1)}, u32[]{:S(2)}, u32[]{:S(2)}) collective-permute-start(bf16[256,1536]{1,0:T(8,128)(2,1)S(1)} %get-tuple-element.303), channel_id=1, source_target_pairs={{0,4},{2,6},{4,0},{6,2},{1,5},{3,7},{5,1},{7,3},{8,12},{10,14},{12... | collective-permute-start | bytes 2359304 | tf_op jit(solution)/shard_map/ppermute | solution.py:444
  440.6 51.5 %collective-permute-start.11 = (bf16[256,1536]{1,0:T(8,128)(2,1)S(1)}, bf16[256,1536]{1,0:T(8,128)(2,1)S(1)}, u32[]{:S(2)}, u32[]{:S(2)}) collective-permute-start(bf16[256,1536]{1,0:T(8,128)(2,1)S(1)} %get-tuple-element.302), channel_id=1, source_target_pairs={{0,2},{2,4},{4,6},{6,0},{1,3},{3,5},{5,7},{7,1},{8,10},{10,12},{12... | collective-permute-start | bytes 2359304 | tf_op jit(solution)/shard_map/ppermute | solution.py:444
  441.7 54.4 %collective-permute-start.9 = (bf16[256,1536]{1,0:T(8,128)(2,1)S(1)}, bf16[256,1536]{1,0:T(8,128)(2,1)S(1)}, u32[]{:S(2)}, u32[]{:S(2)}) collective-permute-start(bf16[256,1536]{1,0:T(8,128)(2,1)S(1)} %get-tuple-element.301), channel_id=1, source_target_pairs={{0,6},{2,0},{4,2},{6,4},{1,7},{3,1},{5,3},{7,5},{8,14},{10,8},{12,... | collective-permute-start | bytes 2359304 | tf_op jit(solution)/shard_map/ppermute | solution.py:444
  452.7 43.4 %copy-start.6 = (f32[256,1536]{1,0:T(8,128)S(1)}, f32[256,1536]{1,0:T(8,128)}, u32[]{:S(2)}) copy-start(f32[256,1536]{1,0:T(8,128)} %copy-done.5) | copy-start | bytes 4718596
  452.8 43.4 %copy-start.66 = (f32[1536]{0:T(1024)S(1)}, f32[1536]{0:T(1024)}, u32[]{:S(2)}) copy-start(f32[1536]{0:T(1024)} %copy-done.65) | copy-start | bytes 18436
  452.9 44.1 %copy-start.81 = (f32[256]{0:T(256)S(1)}, f32[256]{0:T(256)}, u32[]{:S(2)}) copy-start(f32[256]{0:T(256)} %copy-done.80) | copy-start | bytes 3076
  452.9 57.1 %collective-permute-start.3 = (bf16[256,1536]{1,0:T(8,128)(2,1)S(1)}, bf16[256,1536]{1,0:T(8,128)(2,1)S(1)}, u32[]{:S(2)}, u32[]{:S(2)}) collective-permute-start(bf16[256,1536]{1,0:T(8,128)(2,1)S(1)} %get-tuple-element.304), channel_id=1, source_target_pairs={{0,6},{2,0},{4,2},{6,4},{1,7},{3,1},{5,3},{7,5},{8,14},{10,8},{12,... | collective-permute-start | bytes 2359304 | tf_op jit(solution)/shard_map/ppermute | solution.py:444
  453.5 122.4 %collective-permute-start.4 = (bf16[256,1536]{1,0:T(8,128)(2,1)S(1)}, bf16[256,1536]{1,0:T(8,128)(2,1)S(1)}, u32[]{:S(2)}, u32[]{:S(2)}) collective-permute-start(bf16[256,1536]{1,0:T(8,128)(2,1)S(1)} %get-tuple-element.306), channel_id=1, source_target_pairs={{0,4},{2,6},{4,0},{6,2},{1,5},{3,7},{5,1},{7,3},{8,12},{10,14},{12... | collective-permute-start | bytes 2359304 | tf_op jit(solution)/shard_map/ppermute | solution.py:444
  491.7 84.2 %collective-permute-start.5 = (bf16[256,1536]{1,0:T(8,128)(2,1)S(1)}, bf16[256,1536]{1,0:T(8,128)(2,1)S(1)}, u32[]{:S(2)}, u32[]{:S(2)}) collective-permute-start(bf16[256,1536]{1,0:T(8,128)(2,1)S(1)} %get-tuple-element.305), channel_id=1, source_target_pairs={{0,2},{2,4},{4,6},{6,0},{1,3},{3,5},{5,7},{7,1},{8,10},{10,12},{12... | collective-permute-start | bytes 2359304 | tf_op jit(solution)/shard_map/ppermute | solution.py:444
  497.0 82.2 %slice-start = ((s8[4718592]{0:T(1024)(128)(4,1)}), s8[4194304]{0:T(1024)(128)(4,1)S(1)}, s32[]{:S(2)}) async-start(s8[4718592]{0:T(1024)(128)(4,1)} %bitcast.292), calls=%async_computation.3 | async-start | bytes 8388608
  497.0 82.2 %slice-start.1 = ((s8[4718592]{0:T(1024)(128)(4,1)}), s8[524288]{0:T(1024)(128)(4,1)S(1)}, s32[]{:S(2)}) async-start(s8[4718592]{0:T(1024)(128)(4,1)} %bitcast.292), calls=%async_computation.4 | async-start | bytes 1048576
  646.8 81.7 %copy-start.86 = (f32[8,128]{1,0:T(8,128)}, f32[8,128]{1,0:T(8,128)S(1)}, u32[]{:S(2)}) copy-start(f32[8,128]{1,0:T(8,128)S(1)} %reduce_sum.479) | copy-start | bytes 12292
  655.0 74.1 %copy-start.79 = (f32[256]{0:T(256)S(1)}, f32[256]{0:T(256)}, u32[]{:S(2)}) copy-start(f32[256]{0:T(256)} %copy-done.78) | copy-start | bytes 3076
  (103 other events, 903.5 us)
Sparse Core Ops, SparseCore 0:
  132.4 135.2 all-gather.2
  411.8 133.1 reduce-scatter.1
